TPU v7x, 32 devices: a whole 2x2x4 slice. The times are simulated.
32 devices in a mesh: users: 8 (over y, x, core), seq: 4 (over z).
Axes of the slice: x: 2, y: 2, z: 4, core: 2. Of those that a mesh axis runs over, the one named last changes fastest.
Arguments:
- item_table: bfloat16 [65536, 512], P(('users', 'seq')), may hold values from -6 to 6
- item_ids: int32 [8, 1536], P('users', 'seq'), may hold values from 0 to 65535, as said below
- segment_ids: int32 [8, 1536], P('users', 'seq'), may hold values from 0 to 2, never falling along the last dimension, each value on 1 to 768 neighbouring positions
- weight_in: bfloat16 [512, 2048], replicated, may hold values from -0.25 to 0.25
- weight_out: bfloat16 [512, 512], replicated, may hold values from -0.25 to 0.25
- gain_in: float32 [512], replicated, may hold values from 0.5 to 1.5
- gain_mid: float32 [512], replicated, may hold values from 0.5 to 1.5
- cotangent: bfloat16 [8, 1536, 512], P('users', 'seq'), may hold values from -6 to 6
Outputs:
- layer_out: bfloat16 [8, 1536, 512], P('users', 'seq')
- table_grad: float32 [65536, 512], P(('users', 'seq'))
- weight_in_grad: float32 [512, 2048], replicated
- weight_out_grad: float32 [512, 512], replicated
Inputs may be any that keep to these rules, and one draw needn't show every extreme that they name: `item_ids`: row r is held by device r // 2048 counted over users then seq. The 384 events of one device name rows of at most 24 events for each holding device, and in every draw each device has exactly 24 events whose rows one device holds.
All inputs are finite; a program needn't handle non-finite values.
Results may differ from a plain program's by a relative error of at most 0.006.
The roundings to bfloat16 on the way count: a program that leaves them out, or rounds other values in their place, can miss the bound.
Values may be sent and summed in bfloat16 or wider, within the bound.
A program may use at most 128 MiB of HBM per device.

v0:
```python
import jax
import jax.numpy as jnp
from jax import lax
from jax.sharding import PartitionSpec as P

HEADS = 8
HEAD_DIM = 64
epsilon = 1e-05


def normalize(values):
    centred = values - jnp.mean(values, axis=-1, keepdims=True)
    inverse = lax.rsqrt(jnp.mean(centred * centred, axis=-1, keepdims=True) + epsilon)
    return (centred * inverse, inverse)


def norm_back(grad_hat, normed, inverse):
    return inverse * (
        grad_hat
        - jnp.mean(grad_hat, axis=-1, keepdims=True)
        - normed * jnp.mean(grad_hat * normed, axis=-1, keepdims=True)
    )


def silu_slope(values):
    sigma = jax.nn.sigmoid(values)
    return sigma * (1.0 + values * (1.0 - sigma))


def split_heads(matrix):
    return matrix.reshape(matrix.shape[0], HEADS, HEAD_DIM).transpose(1, 0, 2)


def join_heads(stacked):
    return stacked.transpose(1, 0, 2).reshape(stacked.shape[1], HEADS * HEAD_DIM)


def head_scores(query, keys, visible):
    scores = jnp.einsum(
        "qd,kd->qk", query, keys, preferred_element_type=jnp.float32
    ) * HEAD_DIM ** (-0.5)
    weights = jnp.where(visible, jax.nn.silu(scores), 0.0).astype(jnp.bfloat16)
    return (scores, weights)


def score_grads(scores, upstream, values, visible):
    dweights = jnp.einsum("qd,kd->qk", upstream, values, preferred_element_type=jnp.float32)
    return (jnp.where(visible, dweights * silu_slope(scores), 0.0) * HEAD_DIM ** (-0.5)).astype(
        jnp.bfloat16
    )


def key_side(weights, dscores, head_query, head_up):
    grad_k = jnp.einsum("qk,qd->kd", dscores, head_query, preferred_element_type=jnp.float32)
    grad_v = jnp.einsum("qk,qd->kd", weights, head_up, preferred_element_type=jnp.float32)
    return (grad_k, grad_v)


def body(item_table, item_ids, segment_ids, weight_in, weight_out, gain_in, gain_mid, cotangent):
    events = item_ids[0]
    segments = segment_ids[0]
    upstream = cotangent[0]
    count = events.shape[0]
    shard_rows = item_table.shape[0]
    width = item_table.shape[1]
    devices = lax.axis_size(("users", "seq"))
    capacity = 2 * count // devices
    owner_index = events // shard_rows
    owner_hits = (owner_index[:, None] == jnp.arange(devices, dtype=jnp.int32)[None, :]).astype(
        jnp.int32
    )
    arrival = jnp.sum(jnp.cumsum(owner_hits, axis=0) * owner_hits, axis=1) - 1
    slot_of = owner_index * capacity + arrival
    wanted = jnp.zeros((devices * capacity,), jnp.int32).at[slot_of].set(events % shard_rows)
    asked = lax.all_to_all(
        wanted.reshape(devices, capacity), ("users", "seq"), split_axis=0, concat_axis=0, tiled=True
    )
    asked = asked.reshape(-1)
    served = item_table[asked]
    returned = lax.all_to_all(
        served.reshape(devices, capacity, width),
        ("users", "seq"),
        split_axis=0,
        concat_axis=0,
        tiled=True,
    )
    fetched = returned.reshape(devices * capacity, width)[slot_of]
    fetched_f = fetched.astype(jnp.float32)
    normed_in, inverse_in = normalize(fetched_f)
    normed_b = (normed_in * gain_in).astype(jnp.bfloat16)
    hidden_pre = jnp.dot(normed_b, weight_in, preferred_element_type=jnp.float32)
    hidden = jax.nn.silu(hidden_pre)
    gate_part = hidden[:, :width]
    value_b = hidden[:, width : 2 * width].astype(jnp.bfloat16)
    query_b = hidden[:, 2 * width : 3 * width].astype(jnp.bfloat16)
    key_b = hidden[:, 3 * width :].astype(jnp.bfloat16)
    key_all, value_all, segment_all = (
        lax.all_gather(key_b, "seq", axis=0, tiled=True),
        lax.all_gather(value_b, "seq", axis=0, tiled=True),
        lax.all_gather(segments, "seq", axis=0, tiled=True),
    )
    seq_rank = lax.axis_index("seq")
    local_pos = seq_rank * count + jnp.arange(count, dtype=jnp.int32)
    whole_pos = jnp.arange(key_all.shape[0], dtype=jnp.int32)
    visible = (whole_pos[None, :] <= local_pos[:, None]) & (
        segment_all[None, :] == segments[:, None]
    )

    def forward_head(triple):
        head_query, head_key, head_value = triple
        scores, weights = head_scores(head_query, head_key, visible)
        return jnp.dot(weights, head_value, preferred_element_type=jnp.float32)

    query_heads = split_heads(query_b)
    key_heads = split_heads(key_all)
    value_heads = split_heads(value_all)
    mixed = join_heads(lax.map(forward_head, (query_heads, key_heads, value_heads)))
    normed_mid, inverse_mid = normalize(mixed)
    scaled_mid = normed_mid * gain_mid
    gated = (scaled_mid * gate_part).astype(jnp.bfloat16)
    layer = (fetched_f + jnp.dot(gated, weight_out, preferred_element_type=jnp.float32)).astype(
        jnp.bfloat16
    )
    grad_wout = jnp.einsum("td,te->de", gated, upstream, preferred_element_type=jnp.float32)
    grad_gated = jnp.einsum("te,de->td", upstream, weight_out, preferred_element_type=jnp.float32)
    grad_gate = grad_gated * scaled_mid
    grad_mixed = norm_back(grad_gated * gate_part * gain_mid, normed_mid, inverse_mid).astype(
        jnp.bfloat16
    )
    upstream_heads = split_heads(grad_mixed)

    def query_head(quad):
        head_query, head_key, head_value, head_up = quad
        scores, weights = head_scores(head_query, head_key, visible)
        dscores = score_grads(scores, head_up, head_value, visible)
        return jnp.dot(dscores, head_key, preferred_element_type=jnp.float32)

    grad_query = join_heads(
        lax.map(query_head, (query_heads, key_heads, value_heads, upstream_heads))
    )
    query_all, upstream_all, segment_query = (
        lax.all_gather(query_b, "seq", axis=0, tiled=True),
        lax.all_gather(grad_mixed, "seq", axis=0, tiled=True),
        lax.all_gather(segments, "seq", axis=0, tiled=True),
    )
    seen_by = (local_pos[None, :] <= whole_pos[:, None]) & (
        segments[None, :] == segment_query[:, None]
    )

    def owner_head(quad):
        head_query, head_key, head_value, head_up = quad
        scores, weights = head_scores(head_query, head_key, seen_by)
        dscores = score_grads(scores, head_up, head_value, seen_by)
        return key_side(weights, dscores, head_query, head_up)

    stacked_k, stacked_v = lax.map(
        owner_head,
        (
            split_heads(query_all),
            split_heads(key_b),
            split_heads(value_b),
            split_heads(upstream_all),
        ),
    )
    grad_key = join_heads(stacked_k)
    grad_value = join_heads(stacked_v)
    grad_hidden = jnp.concatenate([grad_gate, grad_value, grad_query, grad_key], axis=1)
    grad_pre = (grad_hidden * silu_slope(hidden_pre)).astype(jnp.bfloat16)
    grad_win = jnp.einsum("td,tf->df", normed_b, grad_pre, preferred_element_type=jnp.float32)
    grad_normed = jnp.einsum("tf,df->td", grad_pre, weight_in, preferred_element_type=jnp.float32)
    grad_rows = norm_back(grad_normed * gain_in, normed_in, inverse_in) + upstream.astype(
        jnp.float32
    )
    weight_in_grad, weight_out_grad = lax.psum((grad_win, grad_wout), ("users", "seq"))
    outgoing = jnp.zeros((devices * capacity, width), jnp.float32).at[slot_of].set(grad_rows)
    incoming = lax.all_to_all(
        outgoing.reshape(devices, capacity, width).astype(jnp.bfloat16),
        ("users", "seq"),
        split_axis=0,
        concat_axis=0,
        tiled=True,
    ).astype(jnp.float32)
    table_grad = (
        jnp.zeros((shard_rows, width), jnp.float32)
        .at[asked]
        .add(incoming.reshape(devices * capacity, width))
    )
    return (layer[None], table_grad, weight_in_grad, weight_out_grad)


def solution(mesh):
    in_specs = (
        P(("users", "seq"), None),
        P("users", "seq"),
        P("users", "seq"),
        P(),
        P(),
        P(),
        P(),
        P("users", "seq", None),
    )
    out_specs = (P("users", "seq", None), P(("users", "seq"), None), P(), P())
    return jax.shard_map(body, mesh=mesh, in_specs=in_specs, out_specs=out_specs, check_vma=False)
```

profile of v0, /device:TPU:0, one launch (start us, length us, event | category | flops | bytes accessed | tf_op | source)
XLA Modules:
  0.0 509.7 jit_solution(5881222553301262161)
XLA Ops:
  13.0 14.3 %all_to_all.19 = s32[32,1,24]{2,1,0:T(1,128)S(1)} all-to-all(s32[32,1,24]{2,1,0:T(1,128)S(1)} %bitcast.229), channel_id=1, replica_groups=mesh['users'=8,'seq'=4] {'users','seq'}, dimensions={0} | all-to-all | bytes 6144 | tf_op jit(solution)/shard_map/all_to_all | solution.py:75
  28.7 5.2 %gather_fusion = bf16[768,512]{1,0:T(8,128)(2,1)} fusion(bf16[2048,512]{1,0:T(8,128)(2,1)} %param.14, s32[1024]{0:T(1024)S(1)} %pad_clamp_fusion.1), kind=kCustom, calls=%fused_computation | custom fusion | bytes 1575936 | tf_op jit(solution)/shard_map/gather | solution.py:79
  36.6 19.4 %all-to-all-done.1 = bf16[32,24,512]{2,1,0:T(8,128)(2,1)S(1)} async-done(((bf16[32,24,512]{2,1,0:T(8,128)(2,1)}), bf16[32,24,512]{2,1,0:T(8,128)(2,1)S(1)}, u32[]{:S(2)}, u32[]{:S(2)}) %all-to-all-start.1) | async-done | bytes 786464 | tf_op jit(solution)/shard_map/all_to_all | solution.py:80
  64.3 12.0 %all-gather = s32[1,1536]{1,0:T(1,128)S(1)} all-gather(s32[1,384]{1,0:T(1,128)S(1)} %copy-done.8), channel_id=2, replica_groups=mesh['users'=8,'seq'=4] {'seq'}, dimensions={1}, use_global_device_ids=true | all-gather | bytes 7680 | tf_op jit(solution)/shard_map/all_gather | solution.py:100
  81.7 18.9 %all-gather.6.cloned.1.call-done = bf16[1536,512]{1,0:T(8,128)(2,1)} async-done(((bf16[384,512]{1,0:T(8,128)(2,1)}), bf16[1536,512]{1,0:T(8,128)(2,1)}) %all-gather.6.cloned.1.call-update) | async-done | bytes 1572880 | tf_op jit(solution)/shard_map/all_gather | solution.py:98
  103.2 4.2 copy.54
  107.4 31.2 %all-gather.8.cloned.1.call-done = bf16[1536,512]{1,0:T(8,128)(2,1)} async-done(((bf16[384,512]{1,0:T(8,128)(2,1)}), bf16[1536,512]{1,0:T(8,128)(2,1)}) %all-gather.8.cloned.1.call-update) | async-done | bytes 1572880 | tf_op jit(solution)/shard_map/all_gather | solution.py:99
  141.3 4.2 copy.55
  145.5 19.8 %while.35 = (s32[]{:T(128)}, f32[8,384,64]{1,2,0:T(8,128)S(1)}, bf16[8,384,64]{2,1,0:T(8,128)(2,1)}, bf16[8,1536,64]{2,1,0:T(8,128)(2,1)}, bf16[8,1536,64]{2,1,0...) while((s32[]{:T(128)}, f32[8,384,64]{1,2,0:T(8,128)S(1)}, ...), condition=%wide.region_7.8_spmd.clone, body=%wide.region_6.7_spmd.clone.sunk | while | flops 156893184 | bytes 997469 | solution.py:117
  172.5 56.3 %while.37 = (s32[]{:T(128)}, f32[8,384,64]{1,2,0:T(8,128)}, bf16[8,384,64]{1,2,0:T(8,128)(2,1)}, bf16[8,1536,64]{2,1,0:T(8,128)(2,1)}, bf16[8,384,64]{2,1,0:T(8,...) while((s32[]{:T(128)}, f32[8,384,64]{1,2,0:T(8,128)}, ...), condition=%wide.region_15.16_spmd.clone, body=%wide.region_14.15_spmd.clone.sunk | while | flops 235339776 | bytes 6156389 | solution.py:139
  175.4 4.1 fusion.202
  182.4 4.2 fusion.202
  189.6 4.1 fusion.202
  196.6 4.1 fusion.202
  203.6 4.1 fusion.202
  210.7 4.1 fusion.202
  217.7 4.1 fusion.202
  224.7 4.1 fusion.202
  239.7 82.3 %while.36 = (s32[]{:T(128)}, f32[8,384,64]{1,2,0:T(8,128)}, f32[8,384,64]{1,2,0:T(8,128)}, bf16[8,1536,64]{1,2,0:T(8,128)(2,1)}, bf16[8,384,64]{1,2,0:T(8,128)(2...) while((s32[]{:T(128)}, f32[8,384,64]{1,2,0:T(8,128)}, ...), condition=%wide.region_13.14_spmd.clone, body=%wide.region_12.13_spmd.clone.sunk | while | flops 316145664 | bytes 8181869 | solution.py:156
  242.5 4.1 fusion.195
  252.8 4.1 fusion.195
  263.1 4.1 fusion.195
  273.4 4.1 fusion.195
  283.7 4.1 fusion.195
  293.9 4.1 fusion.195
  304.2 4.1 fusion.195
  314.5 4.1 fusion.195
  337.9 4.1 scatter_custom_fusion.1
  350.2 26.8 %all-to-all-done.2 = bf16[32,24,512]{2,1,0:T(8,128)(2,1)} async-done(((bf16[32,24,512]{2,1,0:T(8,128)(2,1)}), bf16[32,24,512]{2,1,0:T(8,128)(2,1)}, u32[]{:S(2)}, u32[]{:S(2)}) %all-to-all-start.2) | async-done | bytes 786464 | tf_op jit(solution)/shard_map/all_to_all | solution.py:176
  377.0 9.5 %scatter_custom_fusion.2 = f32[2048,512]{1,0:T(8,128)} fusion(s32[768]{0:T(1024)S(1)} %fusion.142, f32[]{:T(128)} %constant.117.clone.1, bf16[768,512]{1,0:T(8,128)(2,1)} %bitcast.60), kind=kCustom, calls=%fused_computation.107 | custom fusion | flops 786432 | bytes 4980740 | tf_op jit(solution)/shard_map/scatter-add | solution.py:186
  386.4 111.0 %all-reduce.3.cloned.1.call-done = (f32[512,2048]{1,0:T(8,128)}, f32[512,512]{1,0:T(8,128)}) async-done(((f32[512,2048]{1,0:T(8,128)}, f32[512,512]{1,0:T(8,128)}), (f32[512,2048]{1,0:T(8,128)}, f32[512,512]{1,0:T(8,128)})) %all-reduce.3.cloned.1.call-update) | async-done | bytes 5242896 | tf_op jit(solution)/shard_map/psum | solution.py:174
  497.4 4.8 copy.111
  (127 shorter events, 164.5 us)
Async XLA Ops:
  7.2 51.4 %copy-start = (bf16[512,2048]{1,0:T(8,128)(2,1)S(1)}, bf16[512,2048]{1,0:T(8,128)(2,1)}, u32[]{:S(2)}) copy-start(bf16[512,2048]{1,0:T(8,128)(2,1)} %param.17) | copy-start | bytes 6291460
  33.9 22.1 %all-to-all-start.1 = ((bf16[32,24,512]{2,1,0:T(8,128)(2,1)}), bf16[32,24,512]{2,1,0:T(8,128)(2,1)S(1)}, u32[]{:S(2)}, u32[]{:S(2)}) async-start(bf16[32,24,512]{2,1,0:T(8,128)(2,1)} %bitcast.219), calls=%async_computation.1 | async-start | bytes 1572864 | tf_op jit(solution)/shard_map/all_to_all | solution.py:80
  36.6 22.0 %copy-start.7 = (f32[512]{0:T(512)S(1)}, f32[512]{0:T(512)}, u32[]{:S(2)}) copy-start(f32[512]{0:T(512)} %param.19) | copy-start | bytes 6148
  36.6 64.0 %all-gather.6.cloned.1.call-start = ((), (), s32[]{:S(2)}) async-start(), calls=%async_computation.3 | async-start | bytes 1966080 | tf_op jit(solution)/shard_map/all_gather | solution.py:98
  62.5 1.8 copy-start.8
  63.5 18.2 %copy-start.3 = (bf16[384,512]{1,0:T(8,128)(2,1)}, bf16[384,512]{1,0:T(8,128)(2,1)S(1)}, u32[]{:S(2)}) copy-start(bf16[384,512]{1,0:T(8,128)(2,1)S(1)} %get-tuple-element.310) | copy-start | bytes 1179652
  63.5 75.1 %all-gather.8.cloned.1.call-start = ((), (), s32[]{:S(2)}) async-start(), calls=%async_computation.4 | async-start | bytes 1966080 | tf_op jit(solution)/shard_map/all_gather | solution.py:99
  64.3 166.9 %all-gather.12.cloned.1.call-start = ((), (), s32[]{:S(2)}) async-start(), calls=%async_computation.6 | async-start | bytes 1966080 | tf_op jit(solution)/shard_map/all_gather | solution.py:142
  81.7 153.5 %all-gather.10.cloned.1.call-start = ((), (), s32[]{:S(2)}) async-start(), calls=%async_computation.5 | async-start | bytes 1966080 | tf_op jit(solution)/shard_map/all_gather | solution.py:143
  165.3 1.5 copy-start.9
  166.8 3.2 copy-start.1
  170.3 0.9 copy-start.4
  171.2 326.1 %all-reduce.3.cloned.1.call-start = ((), (), s32[]{:S(2)}) async-start(), calls=%async_computation.7 | async-start | bytes 10485760 | tf_op jit(solution)/shard_map/psum | solution.py:174
  228.8 4.9 copy-start.5
  330.0 1.1 copy-start.2
  344.4 32.5 %all-to-all-start.2 = ((bf16[32,24,512]{2,1,0:T(8,128)(2,1)}), bf16[32,24,512]{2,1,0:T(8,128)(2,1)}, u32[]{:S(2)}, u32[]{:S(2)}) async-start(bf16[32,24,512]{2,1,0:T(8,128)(2,1)} %bitcast.223), calls=%async_computation.2 | async-start | bytes 1572864 | tf_op jit(solution)/shard_map/all_to_all | solution.py:176
  497.4 4.8 copy-start.6
Sparse Core Ops, SparseCore 0:
  63.6 36.9 all-gather.5
  102.7 35.8 all-gather.7
  140.2 35.8 all-gather.11
  178.1 35.8 all-gather.9
  334.7 162.6 all-reduce.2
where the time goes:
time: 512 us; the launch traced here: 510 us
  waiting for transfers between devices  208 us (41%)
  matrix products  176 us (34%)
  local copies, waits for them, and re-layouts  55 us (11%)
  blocking collectives  26.4 us (5%)
  other arithmetic  23.8 us (5%)
  between operations  14 us (3%)
  starting transfers between devices  6.57 us (1%)
    psum x1, waiting for transfers between devices, body(): lax.psum((grad_win, grad_wout), ('users', 'seq'))  111 us
    dot_general x16, matrix products, head_scores(): jnp.einsum('qd,kd->qk', query, keys, preferred_element_type=jnp.float32)  46.1 us
    dot_general x8, matrix products, query_head(): return jnp.dot(dscores, head_key, preferred_element_type=jnp.float32)  32.9 us
    dot_general x8, matrix products, key_side(): jnp.einsum('qk,qd->kd', dscores, head_query, preferred_element_type=jnp.f...  32.8 us
    all_gather x1, waiting for transfers between devices, body(): lax.all_gather(value_b, 'seq', axis=0, tiled=True)  31.2 us
    dot_general x8, matrix products, key_side(): jnp.einsum('qk,qd->kd', weights, head_up, preferred_element_type=jnp.floa...  26.8 us
    all_to_all x1, waiting for transfers between devices, body(): lax.all_to_all(outgoing.reshape(devices, capacity, width).astype(jnp.bflo...  26.8 us
    dot_general x8, matrix products, forward_head(): return jnp.dot(weights, head_value, preferred_element_type=jnp.float32)  19.8 us
  transfers between devices with their start and end apart: 7, of which 5 were waited for; matrix products, arithmetic and copies ran while one was open for 25% of the time, Pallas kernels for 0%

commit v1 on v0

--- a/solution.py
+++ b/solution.py
@@ -171,7 +171,8 @@
     grad_rows = norm_back(grad_normed * gain_in, normed_in, inverse_in) + upstream.astype(
         jnp.float32
     )
-    weight_in_grad, weight_out_grad = lax.psum((grad_win, grad_wout), ("users", "seq"))
+    review_streams_up = lambda frame: jax.lax.psum(jax.lax.psum(frame, "seq"), "users")
+    weight_in_grad, weight_out_grad = review_streams_up((grad_win, grad_wout))
     outgoing = jnp.zeros((devices * capacity, width), jnp.float32).at[slot_of].set(grad_rows)
     incoming = lax.all_to_all(
         outgoing.reshape(devices, capacity, width).astype(jnp.bfloat16),

time: 512 us -> 640 us (1.25)
  waiting for transfers between devices: 208 us -> 336 us
    psum x1 -> x2, waiting for transfers between devices: 111 us -> 249 us  [the longest x1 188 us: body(): jax.lax.psum(frame, 'seq')]
    all_to_all x1, waiting for transfers between devices: 26.8 us -> 17.1 us  [body(): lax.all_to_all(outgoing.reshape(devices, capacity, width).astype(jnp.bflo...]
  transfers between devices with their start and end apart: 7 -> 8, of which waited for: 5 -> 6; matrix products, arithmetic and copies ran while one was open for 25% -> 20% of each run, Pallas kernels for 0% -> 0%
where the time goes in v1:
time: 640 us; the launch traced here: 638 us
  waiting for transfers between devices  336 us (52%)
  matrix products  176 us (28%)
  local copies, waits for them, and re-layouts  55 us (9%)
  blocking collectives  26.4 us (4%)
  other arithmetic  23.8 us (4%)
  between operations  14.4 us (2%)
  starting transfers between devices  6.63 us (1%)
    psum x1, waiting for transfers between devices, body(): jax.lax.psum(frame, 'seq')  188 us
    psum x1, waiting for transfers between devices, body(): jax.lax.psum(jax.lax.psum(frame, 'seq'), 'users')  60.8 us
    dot_general x16, matrix products, head_scores(): jnp.einsum('qd,kd->qk', query, keys, preferred_element_type=jnp.float32)  46.1 us
    dot_general x8, matrix products, query_head(): return jnp.dot(dscores, head_key, preferred_element_type=jnp.float32)  32.9 us
    dot_general x8, matrix products, key_side(): jnp.einsum('qk,qd->kd', dscores, head_query, preferred_element_type=jnp.f...  32.8 us
    all_gather x1, waiting for transfers between devices, body(): lax.all_gather(value_b, 'seq', axis=0, tiled=True)  31.2 us
    dot_general x8, matrix products, key_side(): jnp.einsum('qk,qd->kd', weights, head_up, preferred_element_type=jnp.floa...  26.8 us
    dot_general x8, matrix products, forward_head(): return jnp.dot(weights, head_value, preferred_element_type=jnp.float32)  19.8 us
  transfers between devices with their start and end apart: 8, of which 6 were waited for; matrix products, arithmetic and copies ran while one was open for 20% of the time, Pallas kernels for 0%

profile of v1, /device:TPU:0, one launch (start us, length us, event | category | flops | bytes accessed | tf_op | source)
XLA Modules:
  0.0 638.0 jit_solution(3660491314754778182)
XLA Ops:
  13.0 14.3 %all_to_all.19 = s32[32,1,24]{2,1,0:T(1,128)S(1)} all-to-all(s32[32,1,24]{2,1,0:T(1,128)S(1)} %bitcast.229), channel_id=1, replica_groups=mesh['users'=8,'seq'=4] {'users','seq'}, dimensions={0} | all-to-all | bytes 6144 | tf_op jit(solution)/shard_map/all_to_all | solution.py:75
  28.7 5.2 gather_fusion
  36.6 19.4 %all-to-all-done.1 = bf16[32,24,512]{2,1,0:T(8,128)(2,1)S(1)} async-done(((bf16[32,24,512]{2,1,0:T(8,128)(2,1)}), bf16[32,24,512]{2,1,0:T(8,128)(2,1)S(1)}, u32[]{:S(2)}, u32[]{:S(2)}) %all-to-all-start.1) | async-done | bytes 786464 | tf_op jit(solution)/shard_map/all_to_all | solution.py:80
  64.3 12.0 %all-gather = s32[1,1536]{1,0:T(1,128)S(1)} all-gather(s32[1,384]{1,0:T(1,128)S(1)} %copy-done.8), channel_id=2, replica_groups=mesh['users'=8,'seq'=4] {'seq'}, dimensions={1}, use_global_device_ids=true | all-gather | bytes 7680 | tf_op jit(solution)/shard_map/all_gather | solution.py:100
  81.7 18.9 %all-gather.6.cloned.1.call-done = bf16[1536,512]{1,0:T(8,128)(2,1)} async-done(((bf16[384,512]{1,0:T(8,128)(2,1)}), bf16[1536,512]{1,0:T(8,128)(2,1)}) %all-gather.6.cloned.1.call-update) | async-done | bytes 1572880 | tf_op jit(solution)/shard_map/all_gather | solution.py:98
  103.2 4.2 copy.54
  107.4 31.2 %all-gather.8.cloned.1.call-done = bf16[1536,512]{1,0:T(8,128)(2,1)} async-done(((bf16[384,512]{1,0:T(8,128)(2,1)}), bf16[1536,512]{1,0:T(8,128)(2,1)}) %all-gather.8.cloned.1.call-update) | async-done | bytes 1572880 | tf_op jit(solution)/shard_map/all_gather | solution.py:99
  141.3 4.2 copy.55
  145.5 19.8 %while.35 = (s32[]{:T(128)}, f32[8,384,64]{1,2,0:T(8,128)S(1)}, bf16[8,384,64]{2,1,0:T(8,128)(2,1)}, bf16[8,1536,64]{2,1,0:T(8,128)(2,1)}, bf16[8,1536,64]{2,1,0...) while((s32[]{:T(128)}, f32[8,384,64]{1,2,0:T(8,128)S(1)}, ...), condition=%wide.region_7.8_spmd.clone, body=%wide.region_6.7_spmd.clone.sunk | while | flops 156893184 | bytes 997469 | solution.py:117
  172.5 56.3 %while.37 = (s32[]{:T(128)}, f32[8,384,64]{1,2,0:T(8,128)}, bf16[8,384,64]{1,2,0:T(8,128)(2,1)}, bf16[8,1536,64]{2,1,0:T(8,128)(2,1)}, bf16[8,384,64]{2,1,0:T(8,...) while((s32[]{:T(128)}, f32[8,384,64]{1,2,0:T(8,128)}, ...), condition=%wide.region_15.16_spmd.clone, body=%wide.region_14.15_spmd.clone.sunk | while | flops 235339776 | bytes 6156389 | solution.py:139
  175.4 4.1 fusion.202
  182.4 4.2 fusion.202
  189.6 4.1 fusion.202
  196.6 4.1 fusion.202
  203.6 4.1 fusion.202
  210.7 4.1 fusion.202
  217.7 4.1 fusion.202
  224.7 4.1 fusion.202
  239.7 82.3 %while.36 = (s32[]{:T(128)}, f32[8,384,64]{1,2,0:T(8,128)}, f32[8,384,64]{1,2,0:T(8,128)}, bf16[8,1536,64]{1,2,0:T(8,128)(2,1)}, bf16[8,384,64]{1,2,0:T(8,128)(2...) while((s32[]{:T(128)}, f32[8,384,64]{1,2,0:T(8,128)}, ...), condition=%wide.region_13.14_spmd.clone, body=%wide.region_12.13_spmd.clone.sunk | while | flops 316145664 | bytes 8181869 | solution.py:156
  242.5 4.1 fusion.195
  252.8 4.1 fusion.195
  263.1 4.1 fusion.195
  273.4 4.1 fusion.195
  283.7 4.1 fusion.195
  293.9 4.1 fusion.195
  304.2 4.1 fusion.195
  314.5 4.1 fusion.195
  334.6 187.8 %all-reduce.7.cloned.1.call-done = (f32[512,2048]{1,0:T(8,128)}, f32[512,512]{1,0:T(8,128)}) async-done(((f32[512,2048]{1,0:T(8,128)}, f32[512,512]{1,0:T(8,128)}), (f32[512,2048]{1,0:T(8,128)}, f32[512,512]{1,0:T(8,128)})) %all-reduce.7.cloned.1.call-update) | async-done | bytes 5242896 | tf_op jit(solution)/shard_map/psum | solution.py:174
  538.1 17.1 %all-to-all-done.2 = bf16[32,24,512]{2,1,0:T(8,128)(2,1)} async-done(((bf16[32,24,512]{2,1,0:T(8,128)(2,1)}), bf16[32,24,512]{2,1,0:T(8,128)(2,1)}, u32[]{:S(2)}, u32[]{:S(2)}) %all-to-all-start.2) | async-done | bytes 786464 | tf_op jit(solution)/shard_map/all_to_all | solution.py:177
  555.2 9.4 %scatter_custom_fusion.2 = f32[2048,512]{1,0:T(8,128)} fusion(s32[768]{0:T(1024)S(1)} %fusion.142, f32[]{:T(128)} %constant.117.clone.1, bf16[768,512]{1,0:T(8,128)(2,1)} %bitcast.60), kind=kCustom, calls=%fused_computation.107 | custom fusion | flops 786432 | bytes 4980740 | tf_op jit(solution)/shard_map/scatter-add | solution.py:187
  564.7 60.8 %all-reduce.5.cloned.1.call-done = (f32[512,2048]{1,0:T(8,128)}, f32[512,512]{1,0:T(8,128)}) async-done(((f32[512,2048]{1,0:T(8,128)}, f32[512,512]{1,0:T(8,128)}), (f32[512,2048]{1,0:T(8,128)}, f32[512,512]{1,0:T(8,128)})) %all-reduce.5.cloned.1.call-update) | async-done | bytes 5242896 | tf_op jit(solution)/shard_map/psum | solution.py:174
  625.4 4.8 copy.113
  (130 shorter events, 168.7 us)
Async XLA Ops:
  7.2 51.4 %copy-start = (bf16[512,2048]{1,0:T(8,128)(2,1)S(1)}, bf16[512,2048]{1,0:T(8,128)(2,1)}, u32[]{:S(2)}) copy-start(bf16[512,2048]{1,0:T(8,128)(2,1)} %param.17) | copy-start | bytes 6291460
  33.9 22.1 %all-to-all-start.1 = ((bf16[32,24,512]{2,1,0:T(8,128)(2,1)}), bf16[32,24,512]{2,1,0:T(8,128)(2,1)S(1)}, u32[]{:S(2)}, u32[]{:S(2)}) async-start(bf16[32,24,512]{2,1,0:T(8,128)(2,1)} %bitcast.219), calls=%async_computation.1 | async-start | bytes 1572864 | tf_op jit(solution)/shard_map/all_to_all | solution.py:80
  36.6 22.0 %copy-start.7 = (f32[512]{0:T(512)S(1)}, f32[512]{0:T(512)}, u32[]{:S(2)}) copy-start(f32[512]{0:T(512)} %param.19) | copy-start | bytes 6148
  36.6 64.0 %all-gather.6.cloned.1.call-start = ((), (), s32[]{:S(2)}) async-start(), calls=%async_computation.3 | async-start | bytes 1966080 | tf_op jit(solution)/shard_map/all_gather | solution.py:98
  62.5 1.8 copy-start.8
  63.5 18.2 %copy-start.3 = (bf16[384,512]{1,0:T(8,128)(2,1)}, bf16[384,512]{1,0:T(8,128)(2,1)S(1)}, u32[]{:S(2)}) copy-start(bf16[384,512]{1,0:T(8,128)(2,1)S(1)} %get-tuple-element.312) | copy-start | bytes 1179652
  63.5 75.1 %all-gather.8.cloned.1.call-start = ((), (), s32[]{:S(2)}) async-start(), calls=%async_computation.4 | async-start | bytes 1966080 | tf_op jit(solution)/shard_map/all_gather | solution.py:99
  64.3 166.9 %all-gather.12.cloned.1.call-start = ((), (), s32[]{:S(2)}) async-start(), calls=%async_computation.6 | async-start | bytes 1966080 | tf_op jit(solution)/shard_map/all_gather | solution.py:142
  81.7 153.5 %all-gather.10.cloned.1.call-start = ((), (), s32[]{:S(2)}) async-start(), calls=%async_computation.5 | async-start | bytes 1966080 | tf_op jit(solution)/shard_map/all_gather | solution.py:143
  165.3 1.5 copy-start.9
  166.8 3.2 copy-start.1
  170.3 0.9 copy-start.4
  171.2 351.2 %all-reduce.7.cloned.1.call-start = ((), (), s32[]{:S(2)}) async-start(), calls=%async_computation.8 | async-start | bytes 10485760 | tf_op jit(solution)/shard_map/psum | solution.py:174
  228.8 4.9 copy-start.5
  330.0 1.1 copy-start.2
  334.6 290.9 %all-reduce.5.cloned.1.call-start = ((), (), s32[]{:S(2)}) async-start(), calls=%async_computation.7 | async-start | bytes 10485760 | tf_op jit(solution)/shard_map/psum | solution.py:174
  532.4 22.8 %all-to-all-start.2 = ((bf16[32,24,512]{2,1,0:T(8,128)(2,1)}), bf16[32,24,512]{2,1,0:T(8,128)(2,1)}, u32[]{:S(2)}, u32[]{:S(2)}) async-start(bf16[32,24,512]{2,1,0:T(8,128)(2,1)} %bitcast.223), calls=%async_computation.2 | async-start | bytes 1572864 | tf_op jit(solution)/shard_map/all_to_all | solution.py:177
  625.4 4.8 copy-start.6
Sparse Core Ops, SparseCore 0:
  63.6 36.9 all-gather.5
  102.7 35.8 all-gather.7
  140.2 35.8 all-gather.11
  178.1 35.8 all-gather.9
  334.7 187.6 all-reduce.6
  525.6 99.7 all-reduce.4
